TPU v7x, 512 devices: a whole 4x4x16 slice. The times are simulated.
512 devices in a mesh: leaf: 16 (over z), col: 32 (over y, x, core).
Axes of the slice: x: 4, y: 4, z: 16, core: 2. Of those that a mesh axis runs over, the one named last changes fastest.
Arguments:
- leaf_solution: float32 [16, 16384, 256], P('leaf', 'col'), may hold values from -6 to 6
- coupling: float32 [16, 768, 128, 128], P('leaf', 'col'), may hold values from -0.01953125 to 0.01953125
- tile_slot: int32 [16, 768], P('leaf', 'col'), may hold values from 0 to 63, as said below
- sep_rhs: float32 [2048, 256], P('col'), may hold values from -6 to 6
- pivot_inverse: float32 [16, 128, 128], P('leaf'), as said below
Outputs:
- sep_solution: float32 [2048, 256], P('col')
- leaf_update: float32 [16, 16384, 256], P('leaf', 'col')
Inputs may be any that keep to these rules, and one draw needn't show every extreme that they name: `tile_slot`: within each aligned block of 24 entries along dimension 1 the values are distinct. `pivot_inverse`: each block is symmetric.
All inputs are finite; a program needn't handle non-finite values.
Results may differ from a plain program's by a relative error of at most 0.0003.
Values sent between devices are 32-bit elements; how exact they have to be, the bound alone decides.
No kernel may reach another device: no remote copies, remote signals or barrier semaphores. Data moves between devices by JAX's collectives and lax.ppermute only.
A program may use at most 64 MiB of HBM per device.

v0:
```python
import jax
import jax.numpy as jnp
from jax import lax
from jax.sharding import PartitionSpec as P


def on_device(leaf_solution, coupling, tile_slot, sep_rhs, pivot_inverse):
    precise = lax.Precision.HIGHEST
    tile_size = coupling.shape[-1]
    rhs_count = leaf_solution.shape[-1]
    leaf_rows = leaf_solution.shape[1]
    col_blocks = leaf_rows // tile_size
    own_rows = sep_rhs.shape[0]
    sep_rows = own_rows * lax.axis_size("col")
    row_blocks = sep_rows // tile_size
    tile_data = coupling[0]
    slot_ids = tile_slot[0]
    tile_row = slot_ids // col_blocks
    tile_col = slot_ids % col_blocks
    leaf_blocks = leaf_solution[0].reshape(col_blocks, tile_size, rhs_count)
    picked = leaf_blocks[tile_col]
    products = jnp.einsum("tij,tjk->tik", tile_data, picked, precision=precise)
    row_hot = (tile_row[None, :] == jnp.arange(row_blocks, dtype=jnp.int32)[:, None]).astype(
        jnp.float32
    )
    partial_value = -jnp.einsum("nt,tik->nik", row_hot, products, precision=precise).reshape(
        sep_rows, rhs_count
    )
    rhs_term = jnp.where(lax.axis_index("leaf") == 0, sep_rhs, jnp.zeros_like(sep_rhs))
    placed = lax.dynamic_update_slice_in_dim(
        jnp.zeros_like(partial_value), rhs_term, lax.axis_index("col") * own_rows, 0
    )
    partial_value = partial_value + placed
    summed = lax.psum(partial_value, ("leaf", "col"))
    pivots = lax.all_gather(pivot_inverse, "leaf", axis=0, tiled=True)
    solved = jnp.einsum(
        "bij,bjk->bik", pivots, summed.reshape(row_blocks, tile_size, rhs_count), precision=precise
    )
    solution = solved.reshape(sep_rows, rhs_count)
    sep_blocks = solution.reshape(row_blocks, tile_size, rhs_count)
    chosen = sep_blocks[tile_row]
    transposed = jnp.einsum("tij,tik->tjk", tile_data, chosen, precision=precise)
    col_hot = (tile_col[None, :] == jnp.arange(col_blocks, dtype=jnp.int32)[:, None]).astype(
        jnp.float32
    )
    update = jnp.einsum("ct,tjk->cjk", col_hot, transposed, precision=precise)
    leaf_update = (leaf_blocks - update).reshape(1, leaf_rows, rhs_count)
    sep_solution = lax.dynamic_slice_in_dim(solution, lax.axis_index("col") * own_rows, own_rows, 0)
    return (sep_solution, leaf_update)


def solution(mesh):
    return jax.shard_map(
        on_device,
        mesh=mesh,
        in_specs=(
            P("leaf", "col", None),
            P("leaf", "col", None, None),
            P("leaf", "col"),
            P("col", None),
            P("leaf", None, None),
        ),
        out_specs=(P("col", None), P("leaf", "col", None)),
        check_vma=False,
    )
```

profile of v0, /device:TPU:1, one launch (start us, length us, event | category | flops | bytes accessed | tf_op | source)
XLA Modules:
  0.0 554.2 jit_solution(7920181868726836255)
XLA Ops:
  8.0 0.0 copy-start
  8.0 0.0 all-reduce.2.cloned.1.call-start
  8.1 0.8 fusion.11
  8.8 0.7 fusion.9
  9.5 3.5 gather_fusion
  13.0 8.3 %convolution_bitcast_fusion.1 = f32[24,128,256]{1,2,0:T(8,128)} fusion(f32[24,128,256]{2,1,0:T(8,128)} %gather_fusion, f32[1,24,128,128]{3,2,1,0:T(8,128)S(1)} %copy-done), kind=kOutput, calls=%fused_computation.3 | convolution fusion | flops 1207959552 | bytes 7864320 | tf_op jit(solution)/shard_map/tij,tjk->tik/dot_general | solution.py:22
  21.3 3.6 copy.18
  24.8 3.3 convolution_negate_fusion
  28.1 0.0 copy-start.3
  28.1 2.5 copy.19
  30.6 1.5 add_dynamic-update-slice_fusion
  32.1 0.0 all-reduce.2.cloned.1.call-update
  32.1 0.2 all-gather.2.cloned.1.call-start
  32.4 0.3 all-gather.2.cloned.1.call-update
  32.7 488.4 %all-reduce.2.cloned.1.call-done = f32[16,128,256]{2,1,0:T(8,128)} async-done(((f32[16,128,256]{2,1,0:T(8,128)}), f32[16,128,256]{2,1,0:T(8,128)}) %all-reduce.2.cloned.1.call-update) | async-done | bytes 2097168 | tf_op jit(solution)/shard_map/psum | solution.py:34
  521.1 3.8 fusion.13
  525.0 0.0 copy-start.2
  525.0 1.3 copy-done.2
  526.3 0.6 constant_dynamic-slice_fusion
  526.9 4.0 gather_fusion.1
  530.9 8.3 %convolution_bitcast_fusion = f32[24,128,256]{1,2,0:T(8,128)} fusion(f32[24,128,256]{2,1,0:T(8,128)} %gather_fusion.1, f32[1,24,128,128]{3,2,1,0:T(8,128)S(1)} %copy-done), kind=kOutput, calls=%fused_computation.2 | convolution fusion | flops 1207959552 | bytes 7864320 | tf_op jit(solution)/shard_map/tij,tik->tjk/dot_general | solution.py:42
  539.2 3.6 copy.21
  542.7 3.2 fusion.6
  545.9 0.9 copy_subtract_fusion
  (7 shorter events, 0.0 us)
Async XLA Ops:
  8.0 5.0 copy-start
  8.0 513.1 %all-reduce.2.cloned.1.call-start = ((), (), s32[]{:S(2)}) async-start(), calls=%async_computation | async-start | bytes 4194304 | tf_op jit(solution)/shard_map/psum | solution.py:34
  28.1 2.5 copy-start.3
  32.1 489.0 %all-gather.2.cloned.1.call-start = ((), (), s32[]{:S(2)}) async-start(), calls=%async_computation.1 | async-start | bytes 1114112 | tf_op jit(solution)/shard_map/all_gather | solution.py:35
  525.0 1.3 copy-start.2
  542.7 3.2 copy-start.1
Sparse Core Ops, SparseCore 0:
  32.3 488.7 all-reduce.1
Sparse Core Ops, SparseCore 1:
  34.7 66.8 all-gather.1
where the time goes:
time: 555 us; the launch traced here: 554 us
  waiting for transfers between devices  489 us (88%)
  matrix products  26.8 us (5%)
  local copies, waits for them, and re-layouts  19.1 us (3%)
  between operations  15.5 us (3%)
    psum x1, waiting for transfers between devices, on_device(): summed = lax.psum(partial_value, ('leaf', 'col'))  488 us
  transfers between devices with their start and end apart: 2, of which 1 were waited for; matrix products, arithmetic and copies ran while one was open for 0% of the time, Pallas kernels for 0%

commit v1 on v0

--- a/solution.py
+++ b/solution.py
@@ -31,7 +31,8 @@
         jnp.zeros_like(partial_value), rhs_term, lax.axis_index("col") * own_rows, 0
     )
     partial_value = partial_value + placed
-    summed = lax.psum(partial_value, ("leaf", "col"))
+    one_axis = lax.psum(partial_value, "leaf")
+    summed = lax.psum(one_axis, "col")
     pivots = lax.all_gather(pivot_inverse, "leaf", axis=0, tiled=True)
     solved = jnp.einsum(
         "bij,bjk->bik", pivots, summed.reshape(row_blocks, tile_size, rhs_count), precision=precise

time: 555 us -> 422 us (0.76)
  waiting for transfers between devices: 489 us -> 358 us
    psum x1 -> x2, waiting for transfers between devices: 488 us -> 288 us  [the longest x1 149 us: on_device(): summed = lax.psum(one_axis, 'col')]
    all_gather x1, waiting for transfers between devices: 0.01 us -> 68.8 us  [on_device(): pivots = lax.all_gather(pivot_inverse, 'leaf', axis=0, tiled=True)]
  transfers between devices with their start and end apart: 2 -> 3, of which waited for: 1 -> 3; matrix products, arithmetic and copies ran while one was open for 0% -> 0% of each run, Pallas kernels for 0% -> 0%
where the time goes in v1:
time: 422 us; the launch traced here: 421 us
  waiting for transfers between devices  358 us (85%)
  matrix products  26.8 us (6%)
  local copies, waits for them, and re-layouts  19.1 us (5%)
  between operations  13.8 us (3%)
    psum x1, waiting for transfers between devices, on_device(): summed = lax.psum(one_axis, 'col')  149 us
    psum x1, waiting for transfers between devices, on_device(): one_axis = lax.psum(partial_value, 'leaf')  139 us
    all_gather x1, waiting for transfers between devices, on_device(): pivots = lax.all_gather(pivot_inverse, 'leaf', axis=0, tiled=True)  68.8 us
  transfers between devices with their start and end apart: 3, of which 3 were waited for; matrix products, arithmetic and copies ran while one was open for 0% of the time, Pallas kernels for 0%

profile of v1, /device:TPU:1, one launch (start us, length us, event | category | flops | bytes accessed | tf_op | source)
XLA Modules:
  0.0 421.5 jit_solution(17871048465799552161)
XLA Ops:
  7.2 0.0 all-reduce.3.cloned.1.call-start
  7.2 0.8 fusion.11
  8.0 0.7 fusion.9
  8.7 3.5 gather_fusion
  12.2 8.3 %convolution_bitcast_fusion.1 = f32[24,128,256]{1,2,0:T(8,128)} fusion(f32[24,128,256]{2,1,0:T(8,128)} %gather_fusion, f32[1,24,128,128]{3,2,1,0:T(8,128)S(1)} %copy-done), kind=kOutput, calls=%fused_computation.3 | convolution fusion | flops 1207959552 | bytes 7864320 | tf_op jit(solution)/shard_map/tij,tjk->tik/dot_general | solution.py:22
  20.4 3.6 copy.18
  24.0 3.3 convolution_negate_fusion
  27.3 2.5 copy.19
  29.8 1.5 add_dynamic-update-slice_fusion
  31.3 0.0 all-reduce.3.cloned.1.call-update
  31.3 0.0 all-gather.2.cloned.1.call-start
  31.4 0.7 all-gather.2.cloned.1.call-update
  32.1 0.2 all-reduce.5.cloned.1.call-start
  32.3 139.3 %all-reduce.3.cloned.1.call-done = f32[2048,256]{1,0:T(8,128)} async-done(((f32[2048,256]{1,0:T(8,128)}), f32[2048,256]{1,0:T(8,128)}) %all-reduce.3.cloned.1.call-update) | async-done | bytes 2097168 | tf_op jit(solution)/shard_map/psum | solution.py:34
  171.7 68.8 %all-gather.2.cloned.1.call-done = f32[16,128,128]{2,1,0:T(8,128)} async-done(((f32[1,128,128]{2,1,0:T(8,128)}), f32[16,128,128]{2,1,0:T(8,128)}) %all-gather.2.cloned.1.call-update) | async-done | bytes 1048592 | tf_op jit(solution)/shard_map/all_gather | solution.py:36
  240.4 148.8 %all-reduce.5.cloned.1.call-done = f32[16,128,256]{2,1,0:T(8,128)} async-done(((f32[16,128,256]{2,1,0:T(8,128)}), f32[16,128,256]{2,1,0:T(8,128)}) %all-reduce.5.cloned.1.call-update) | async-done | bytes 2097168 | tf_op jit(solution)/shard_map/psum | solution.py:35
  389.2 3.8 fusion.13
  393.1 1.3 copy-done.2
  394.4 0.6 constant_dynamic-slice_fusion
  395.1 4.0 gather_fusion.1
  399.0 8.3 %convolution_bitcast_fusion = f32[24,128,256]{1,2,0:T(8,128)} fusion(f32[24,128,256]{2,1,0:T(8,128)} %gather_fusion.1, f32[1,24,128,128]{3,2,1,0:T(8,128)S(1)} %copy-done), kind=kOutput, calls=%fused_computation.2 | convolution fusion | flops 1207959552 | bytes 7864320 | tf_op jit(solution)/shard_map/tij,tik->tjk/dot_general | solution.py:43
  407.3 3.6 copy.21
  410.9 3.2 fusion.6
  414.0 0.9 copy_subtract_fusion
  (10 shorter events, 0.0 us)
Async XLA Ops:
  7.2 5.0 %copy-start = (f32[1,24,128,128]{3,2,1,0:T(8,128)S(1)}, f32[1,24,128,128]{3,2,1,0:T(8,128)}, u32[]{:S(2)}) copy-start(f32[1,24,128,128]{3,2,1,0:T(8,128)} %param.6) | copy-start | bytes 4718596
  7.2 164.4 %all-reduce.3.cloned.1.call-start = ((), (), s32[]{:S(2)}) async-start(), calls=%async_computation | async-start | bytes 4194304 | tf_op jit(solution)/shard_map/psum | solution.py:34
  27.3 2.5 copy-start.3
  31.3 209.1 %all-gather.2.cloned.1.call-start = ((), (), s32[]{:S(2)}) async-start(), calls=%async_computation.2 | async-start | bytes 1114112 | tf_op jit(solution)/shard_map/all_gather | solution.py:36
  32.1 357.2 %all-reduce.5.cloned.1.call-start = ((), (), s32[]{:S(2)}) async-start(), calls=%async_computation.1 | async-start | bytes 4194304 | tf_op jit(solution)/shard_map/psum | solution.py:35
  393.1 1.3 copy-start.2
  410.8 3.2 copy-start.1
Sparse Core Ops, SparseCore 0:
  31.4 140.1 all-reduce.2
  173.7 66.6 all-gather.1
  243.7 145.5 all-reduce.4
